TPU v7x, 512 devices: a whole 4x4x16 slice. The times are simulated.
512 devices in a mesh: ctx: 128 (over y_lo, x, z), head: 4 (over y_hi, core).
Axes of the slice: x: 4, y: 4 (y_hi: 2, y_lo: 2; y = y_hi * 2 + y_lo), z: 16, core: 2. Of those that a mesh axis runs over, the one named last changes fastest.
Arguments:
- hidden: bfloat16 [16384, 8192], P('ctx', 'head'), may hold values from -6 to 6
- frozen_query_rows: bfloat16 [16384, 3072], P('ctx', 'head'), may hold values from -101 to 101
- frozen_key_rows: bfloat16 [16384, 256], P('ctx'), may hold values from -5 to 5
- frozen_value_rows: bfloat16 [16384, 256], P('ctx'), may hold values from -6 to 6
- adapter_down_factors: bfloat16 [8192, 64], P('head'), may hold values from -0.0625 to 0.0625
- query_up_factor: bfloat16 [32, 3072], P(None, 'head'), may hold values from -1 to 1
- value_up_factor: bfloat16 [32, 256], replicated, may hold values from -1 to 1
- slot_span_order: int32 [256], replicated, may hold values from 0 to 255, each once
Outputs:
- attended: bfloat16 [16384, 3072], P('ctx', 'head')
- log_normalizer: float32 [24, 16384], P('head', 'ctx')
Inputs may be any that keep to these rules, and one draw needn't show every extreme that they name: `slot_span_order`: every span number appears once.
All inputs are finite; a program needn't handle non-finite values.
Results may differ from a plain program's by a relative error of at most 0.018.
Values may be sent and summed in bfloat16 or wider, within the bound.
A program may use at most 64 MiB of HBM per device.

v0:
```python
import math
import jax
import jax.numpy as jnp
from jax import lax
from jax.sharding import PartitionSpec as P

HEAD_SIZE = 128
KEY_VALUE_HEADS = 2
ADAPTER_RANK = 32
adapter_scale = 0.5
start_max = -1e30


def from_partner(value, axis, stride):
    return lax.ppermute(value, axis, [(i, i ^ 1 << stride) for i in range(lax.axis_size(axis))])


def spread_positions(span_ids, span_len):
    return (span_ids[:, None] * span_len + jnp.arange(span_len, dtype=jnp.int32)[None, :]).reshape(
        -1
    )


def stack_heads(matrix, width):
    return matrix.reshape(matrix.shape[0], -1, width).transpose(1, 0, 2).reshape(-1, width)


def empty_state(row_count, width):
    return (
        jnp.full((row_count,), start_max, jnp.float32),
        jnp.zeros((row_count,), jnp.float32),
        jnp.zeros((row_count, width), jnp.float32),
    )


def update_state(carry_state, query_matrix, query_pos, key_block, value_block, key_pos):
    running_max, denominator, numerator = carry_state
    scores = lax.dot_general(
        query_matrix, key_block, (((1,), (1,)), ((), ())), preferred_element_type=jnp.float32
    ) * (1.0 / math.sqrt(key_block.shape[1]))
    visible = key_pos[None, :] <= query_pos[:, None]
    block_max = jnp.max(jnp.where(visible, scores, -jnp.inf), axis=1)
    new_max = jnp.maximum(running_max, block_max)
    rescale = jnp.exp(running_max - new_max)
    weights = jnp.where(visible, jnp.exp(scores - new_max[:, None]), 0.0)
    denominator = denominator * rescale + jnp.sum(weights, axis=1)
    numerator = numerator * rescale[:, None] + jnp.dot(
        weights.astype(jnp.bfloat16), value_block, preferred_element_type=jnp.float32
    )
    return (new_max, denominator, numerator)


def sweep_keys(carry_state, query_matrix, query_pos, key_rows, value_rows, key_pos):
    key_count = key_rows.shape[0]
    block_len = math.gcd(key_count, 1024)

    def one_block(block_index, inner_state):
        offset = block_index * block_len
        key_block = lax.dynamic_slice_in_dim(key_rows, offset, block_len, 0)
        value_block = lax.dynamic_slice_in_dim(value_rows, offset, block_len, 0)
        pos_block = lax.dynamic_slice_in_dim(key_pos, offset, block_len, 0)
        return update_state(inner_state, query_matrix, query_pos, key_block, value_block, pos_block)

    return lax.fori_loop(0, key_count // block_len, one_block, carry_state)


def merge_states(first_state, second_state):
    first_max, first_total, first_sum = first_state
    second_max, second_total, second_sum = second_state
    new_max = jnp.maximum(first_max, second_max)
    first_scale = jnp.exp(first_max - new_max)
    second_scale = jnp.exp(second_max - new_max)
    return (
        new_max,
        first_total * first_scale + second_total * second_scale,
        first_sum * first_scale[:, None] + second_sum * second_scale[:, None],
    )


def local(
    hidden,
    frozen_query_rows,
    frozen_key_rows,
    frozen_value_rows,
    adapter_down_factors,
    query_up_factor,
    value_up_factor,
    slot_span_order,
):
    tok_dev = hidden.shape[0]
    span_len = tok_dev // 2
    partial_bottleneck = jnp.dot(hidden, adapter_down_factors, preferred_element_type=jnp.float32)
    adapter_bottleneck = lax.psum(partial_bottleneck.astype(jnp.bfloat16), "head")
    query_rows = (
        frozen_query_rows.astype(jnp.float32)
        + adapter_scale
        * jnp.dot(
            adapter_bottleneck[:, :ADAPTER_RANK],
            query_up_factor,
            preferred_element_type=jnp.float32,
        )
    ).astype(jnp.bfloat16)
    head_index = lax.axis_index("head")
    key_value_index = head_index // (lax.axis_size("head") // KEY_VALUE_HEADS)
    key_rows = lax.dynamic_slice_in_dim(frozen_key_rows, key_value_index * HEAD_SIZE, HEAD_SIZE, 1)
    value_base = lax.dynamic_slice_in_dim(
        frozen_value_rows, key_value_index * HEAD_SIZE, HEAD_SIZE, 1
    )
    value_up_update = lax.dynamic_slice_in_dim(
        value_up_factor, key_value_index * HEAD_SIZE, HEAD_SIZE, 1
    )
    value_rows = (
        value_base.astype(jnp.float32)
        + adapter_scale
        * jnp.dot(
            adapter_bottleneck[:, ADAPTER_RANK:],
            value_up_update,
            preferred_element_type=jnp.float32,
        )
    ).astype(jnp.bfloat16)
    span_pairs = slot_span_order.reshape(-1, 2)
    own_spans = lax.dynamic_slice_in_dim(span_pairs, lax.axis_index("ctx"), 1, 0).reshape(2)
    own_positions = spread_positions(own_spans, span_len)
    heads_dev = query_rows.shape[1] // HEAD_SIZE
    query_matrix = stack_heads(query_rows, HEAD_SIZE)
    query_pos = jnp.tile(own_positions, heads_dev)
    own_count = query_matrix.shape[0]
    half_side = head_index % 2
    partner = from_partner(query_matrix, "head", 0)
    stacked = jnp.concatenate([query_matrix, partner], axis=0)
    stacked_pos = jnp.concatenate([query_pos, query_pos])
    key_half = lax.dynamic_slice_in_dim(key_rows, half_side * span_len, span_len, 0)
    value_half = lax.dynamic_slice_in_dim(value_rows, half_side * span_len, span_len, 0)
    span_ids = jnp.where(half_side == 0, span_pairs[:, 0], span_pairs[:, 1])
    running_max, denominator, numerator = sweep_keys(
        empty_state(2 * own_count, HEAD_SIZE),
        stacked,
        stacked_pos,
        lax.all_gather(key_half, "ctx", axis=0, tiled=True),
        lax.all_gather(value_half, "ctx", axis=0, tiled=True),
        spread_positions(span_ids, span_len),
    )
    returned = (
        from_partner(running_max[own_count:].astype(jnp.bfloat16), "head", 0).astype(jnp.float32),
        from_partner(denominator[own_count:].astype(jnp.bfloat16), "head", 0).astype(jnp.float32),
        from_partner(numerator[own_count:].astype(jnp.bfloat16), "head", 0).astype(jnp.float32),
    )
    running_max, denominator, numerator = merge_states(
        (running_max[:own_count], denominator[:own_count], numerator[:own_count]), returned
    )
    result = (numerator / denominator[:, None]).astype(jnp.bfloat16)
    attended = (
        result.reshape(heads_dev, tok_dev, HEAD_SIZE)
        .transpose(1, 0, 2)
        .reshape(tok_dev, heads_dev * HEAD_SIZE)
    )
    log_normalizer = (running_max + jnp.log(denominator)).reshape(heads_dev, tok_dev)
    return (attended, log_normalizer)


def solution(mesh):
    placed = (
        P("ctx", "head"),
        P("ctx", "head"),
        P("ctx", None),
        P("ctx", None),
        P("head", None),
        P(None, "head"),
        P(),
        P(),
    )
    return jax.shard_map(
        local,
        mesh=mesh,
        in_specs=placed,
        out_specs=(P("ctx", "head"), P("head", "ctx")),
        check_vma=False,
    )
```

profile of v0, /device:TPU:1, one launch (start us, length us, event | category | flops | bytes accessed | tf_op | source)
XLA Modules:
  0.0 1264.8 jit_solution(4207218404230548502)
XLA Ops:
  7.2 0.0 copy-start
  7.2 0.0 all-gather.3.cloned.1.call-start
  7.3 1.5 dynamic_slice.38
  8.8 0.0 all-gather.3.cloned.1.call-update
  8.8 0.0 all-gather.5.cloned.1.call-start
  8.8 0.0 copy-done
  8.9 1.3 convolution_convert_fusion
  10.1 16.1 %psum.7 = bf16[128,64]{0,1:T(8,128)(2,1)S(1)} all-reduce(bf16[128,64]{0,1:T(8,128)(2,1)S(1)} %convolution_convert_fusion), channel_id=1, replica_groups=mesh['ctx'=128,'head'=4] {'head'}, use_global_device_ids=true, to_apply=%region_0.0 | all-reduce | flops 8192 | bytes 32768 | tf_op jit(solution)/shard_map/psum | solution.py:93
  26.3 0.9 fusion.24
  27.1 1.3 fusion.23
  28.5 0.0 all-gather.5.cloned.1.call-update
  28.5 1.2 fusion.19
  29.7 0.2 copy.14
  29.9 0.2 copy.15
  30.0 5.7 collective-permute-start
  35.8 0.8 reshape.57
  36.6 0.1 iota_add_fusion.1
  36.7 0.1 add.124
  36.8 0.2 fusion.21
  37.0 0.1 iota_add_fusion
  37.1 0.1 add.119
  37.2 0.0 collective-permute-done
  37.2 477.1 %all-gather.3.cloned.1.call-done = bf16[8192,128]{1,0:T(8,128)(2,1)} async-done(((bf16[64,128]{1,0:T(8,128)(2,1)}), bf16[8192,128]{1,0:T(8,128)(2,1)}) %all-gather.3.cloned.1.call-update) | async-done | bytes 2097168 | tf_op jit(solution)/shard_map/all_gather | solution.py:139
  514.4 585.6 %all-gather.5.cloned.1.call-done = bf16[8192,128]{1,0:T(8,128)(2,1)} async-done(((bf16[64,128]{1,0:T(8,128)(2,1)}), bf16[8192,128]{1,0:T(8,128)(2,1)}) %all-gather.5.cloned.1.call-update) | async-done | bytes 2097168 | tf_op jit(solution)/shard_map/all_gather | solution.py:140
  1099.9 55.1 %while.18 = (s32[]{:T(128)}, f32[1536]{0:T(1024)S(1)}, f32[1536]{0:T(1024)S(1)}, f32[1536,128]{1,0:T(8,128)S(1)}, s32[8192]{0:T(1024)S(1)}, /*index=5*/s32[1536]...) while((s32[]{:T(128)}, f32[1536]{0:T(1024)S(1)}, ...), condition=%wide.region_4.5_spmd.clone, body=%wide.region_1.4_spmd.clone.sunk | while | flops 827923968 | bytes 21502156 | solution.py:64
  1099.9 1.9 fusion.52
  1101.9 1.9 fusion.53
  1103.8 2.9 fusion.55
  1106.8 2.0 fusion.52
  1108.8 1.9 fusion.53
  1110.7 2.9 fusion.55
  1113.7 2.0 fusion.52
  1115.7 1.9 fusion.53
  1117.6 2.9 fusion.55
  1120.6 2.0 fusion.52
  1122.6 1.9 fusion.53
  1124.5 2.9 fusion.55
  1127.5 2.0 fusion.52
  1129.5 1.9 fusion.53
  1131.4 2.9 fusion.55
  1134.4 2.0 fusion.52
  1136.4 1.9 fusion.53
  1138.3 2.9 fusion.55
  1141.3 2.0 fusion.52
  1143.2 1.9 fusion.53
  1145.2 2.9 fusion.55
  1148.1 2.0 fusion.52
  1150.1 1.9 fusion.53
  1152.0 2.9 fusion.55
  1155.0 96.1 %collective-permute-start.3 = (bf16[768]{0:T(1024)(128)(2,1)S(1)}, bf16[768]{0:T(1024)(128)(2,1)S(1)}, u32[]{:S(2)}, u32[]{:S(2)}) collective-permute-start(bf16[768]{0:T(1024)(128)(2,1)S(1)} %slice.69), channel_id=1, source_target_pairs={{0,1},{1,0},{2,3},{3,2},{4,5},{5,4},{6,7},{7,6},{8,9},{9,8},{10,11... | collective-permute-start | bytes 4616 | tf_op jit(solution)/shard_map/ppermute | solution.py:15
  1251.2 1.9 collective-permute-start.1
  1253.1 2.4 collective-permute-start.2
  1255.5 0.0 collective-permute-done.3
  1255.5 0.0 collective-permute-done.1
  1255.5 0.6 fusion.31
  1256.2 0.4 collective-permute-done.2
  1256.6 0.4 divide_convert_fusion
  1256.9 0.2 copy.16
  1257.1 0.8 copy.17
  (42 shorter events, 0.3 us)
Async XLA Ops:
  7.2 1.7 copy-start
  7.2 507.2 %all-gather.3.cloned.1.call-start = ((), (), s32[]{:S(2)}) async-start(), calls=%async_computation | async-start | bytes 2113536 | tf_op jit(solution)/shard_map/all_gather | solution.py:139
  8.8 1091.1 %all-gather.5.cloned.1.call-start = ((), (), s32[]{:S(2)}) async-start(), calls=%async_computation.1 | async-start | bytes 2113536 | tf_op jit(solution)/shard_map/all_gather | solution.py:140
  30.0 7.2 collective-permute-start
  1155.0 100.5 %collective-permute-start.3 = (bf16[768]{0:T(1024)(128)(2,1)S(1)}, bf16[768]{0:T(1024)(128)(2,1)S(1)}, u32[]{:S(2)}, u32[]{:S(2)}) collective-permute-start(bf16[768]{0:T(1024)(128)(2,1)S(1)} %slice.69), channel_id=1, source_target_pairs={{0,1},{1,0},{2,3},{3,2},{4,5},{5,4},{6,7},{7,6},{8,9},{9,8},{10,11... | collective-permute-start | bytes 4616 | tf_op jit(solution)/shard_map/ppermute | solution.py:15
  1251.2 4.4 collective-permute-start.1
  1253.1 3.5 collective-permute-start.2
Sparse Core Ops, SparseCore 0:
  10.6 503.6 all-gather.2
  516.4 583.4 all-gather.4
where the time goes:
time: 1270 us; the launch traced here: 1260 us
  waiting for transfers between devices  1060 us (83%)
  starting transfers between devices  106 us (8%)
  matrix products  42.5 us (3%)
  other arithmetic  17.9 us (1%)
  blocking collectives  16.1 us (1%)
  between operations  14.3 us (1%)
    all_gather x1, waiting for transfers between devices, local(): lax.all_gather(value_half, 'ctx', axis=0, tiled=True)  586 us
    all_gather x1, waiting for transfers between devices, local(): lax.all_gather(key_half, 'ctx', axis=0, tiled=True)  477 us
    ppermute x4, starting transfers between devices, from_partner(): lax.ppermute(value, axis, [(i, i ^ 1 << stride) for i in range(lax.axis_s...  106 us
  transfers between devices with their start and end apart: 6, of which 3 were waited for; matrix products, arithmetic and copies ran while one was open for 1% of the time, Pallas kernels for 0%

commit v1 on v0

--- a/solution.py
+++ b/solution.py
@@ -9,6 +9,13 @@
 ADAPTER_RANK = 32
 adapter_scale = 0.5
 start_max = -1e30
+
+
+def all_by_exchange(x, name, dim):
+    size = lax.axis_size(name)
+    blocks = jnp.stack([x for _ in range(size)])
+    blocks = lax.all_to_all(blocks, name, split_axis=0, concat_axis=0)
+    return jnp.concatenate(blocks, axis=dim)
 
 
 def from_partner(value, axis, stride):
@@ -136,7 +143,7 @@
         empty_state(2 * own_count, HEAD_SIZE),
         stacked,
         stacked_pos,
-        lax.all_gather(key_half, "ctx", axis=0, tiled=True),
+        all_by_exchange(key_half, "ctx", 0),
         lax.all_gather(value_half, "ctx", axis=0, tiled=True),
         spread_positions(span_ids, span_len),
     )

time: 1270 us -> 719 us (0.57)
  waiting for transfers between devices: 1060 us -> 501 us
  starting transfers between devices: 106 us -> 126 us
    all_gather x1 -> x0, waiting for transfers between devices: 477 us -> none  [local(): lax.all_gather(key_half, 'ctx', axis=0, tiled=True)]
    all_gather x1, waiting for transfers between devices: 586 us -> 500 us  [local(): lax.all_gather(value_half, 'ctx', axis=0, tiled=True)]
    all_to_all x0 -> x1, starting transfers between devices: none -> 21.3 us  [all_by_exchange(): blocks = lax.all_to_all(blocks, name, split_axis=0, concat_axis=0)]
where the time goes in v1:
time: 719 us; the launch traced here: 718 us
  waiting for transfers between devices  501 us (70%)
  starting transfers between devices  126 us (18%)
  matrix products  32.3 us (4%)
  other arithmetic  18.9 us (3%)
  between operations  14.3 us (2%)
  blocking collectives  13.4 us (2%)
  local copies, waits for them, and re-layouts  12.5 us (2%)
    all_gather x1, waiting for transfers between devices, local(): lax.all_gather(value_half, 'ctx', axis=0, tiled=True)  500 us
    ppermute x4, starting transfers between devices, from_partner(): lax.ppermute(value, axis, [(i, i ^ 1 << stride) for i in range(lax.axis_s...  104 us
    dot_general x8, matrix products, update_state(): jnp.dot(weights.astype(jnp.bfloat16), value_block, preferred_element_type...  23.5 us
    all_to_all x1, starting transfers between devices, all_by_exchange(): blocks = lax.all_to_all(blocks, name, split_axis=0, concat_axis=0)  21.3 us
    reduce_sum x8, other arithmetic, update_state(): denominator = denominator * rescale + jnp.sum(weights, axis=1)  15 us
  transfers between devices with their start and end apart: 6, of which 3 were waited for; matrix products, arithmetic and copies ran while one was open for 1% of the time, Pallas kernels for 0%

profile of v1, /device:TPU:1, one launch (start us, length us, event | category | flops | bytes accessed | tf_op | source)
XLA Modules:
  0.0 718.0 jit_solution(5876102946501772765)
XLA Ops:
  7.2 0.0 copy-start
  7.3 0.9 dynamic_slice.38
  8.2 1.8 stack.2
  10.0 21.3 %all-to-all-start = ((bf16[128,64,128]{2,1,0:T(8,128)(2,1)}), bf16[128,64,128]{2,1,0:T(8,128)(2,1)S(1)}, u32[]{:S(2)}, u32[]{:S(2)}) async-start(bf16[128,64,128]{2,1,0:T(8,128)(2,1)} %stack.2), calls=%async_computation | async-start | bytes 4194304 | tf_op jit(solution)/shard_map/all_to_all | solution.py:17
  31.4 0.0 all-gather.2.cloned.1.call-start
  31.4 0.3 convolution_convert_fusion
  31.8 13.4 %psum.7 = bf16[128,64]{0,1:T(8,128)(2,1)S(1)} all-reduce(bf16[128,64]{0,1:T(8,128)(2,1)S(1)} %convolution_convert_fusion), channel_id=1, replica_groups=mesh['ctx'=128,'head'=4] {'head'}, use_global_device_ids=true, to_apply=%region_0.0 | all-reduce | flops 8192 | bytes 32768 | tf_op jit(solution)/shard_map/psum | solution.py:100
  45.1 0.2 fusion.24
  45.3 1.3 fusion.23
  46.7 0.0 all-gather.2.cloned.1.call-update
  46.7 0.2 fusion.19
  47.0 0.2 copy.14
  47.1 0.2 copy.15
  47.3 5.1 collective-permute-start
  52.4 0.1 reshape.62
  52.6 0.1 iota_add_fusion.1
  52.7 0.1 add.124
  52.8 0.2 fusion.21
  52.9 0.1 iota_add_fusion
  53.1 0.1 add.119
  53.1 0.3 collective-permute-done
  53.5 499.8 %all-gather.2.cloned.1.call-done = bf16[8192,128]{1,0:T(8,128)(2,1)} async-done(((bf16[64,128]{1,0:T(8,128)(2,1)}), bf16[8192,128]{1,0:T(8,128)(2,1)}) %all-gather.2.cloned.1.call-update) | async-done | bytes 2097168 | tf_op jit(solution)/shard_map/all_gather | solution.py:147
  553.3 54.3 %while.18 = (s32[]{:T(128)}, f32[1536]{0:T(1024)S(1)}, f32[1536]{0:T(1024)S(1)}, f32[1536,128]{1,0:T(8,128)}, s32[8192]{0:T(1024)S(1)}, /*index=5*/s32[1536]{0:T...) while((s32[]{:T(128)}, f32[1536]{0:T(1024)S(1)}, ...), condition=%wide.region_4.5_spmd.clone, body=%wide.region_1.4_spmd.clone.sunk | while | flops 827923968 | bytes 27795716 | solution.py:71
  553.3 1.0 fusion.52
  554.3 1.9 fusion.53
  556.2 2.9 fusion.55
  559.2 0.9 copy-done.2
  560.0 1.0 fusion.52
  561.1 1.9 fusion.53
  563.0 2.9 fusion.55
  566.0 0.9 copy-done.2
  566.8 1.0 fusion.52
  567.9 1.9 fusion.53
  569.8 2.9 fusion.55
  572.8 0.9 copy-done.2
  573.6 1.0 fusion.52
  574.7 1.9 fusion.53
  576.6 2.9 fusion.55
  579.5 0.9 copy-done.2
  580.4 1.0 fusion.52
  581.5 1.9 fusion.53
  583.4 2.9 fusion.55
  586.3 0.9 copy-done.2
  587.2 1.0 fusion.52
  588.2 1.9 fusion.53
  590.2 2.9 fusion.55
  593.1 0.9 copy-done.2
  594.0 1.0 fusion.52
  595.0 1.9 fusion.53
  596.9 2.9 fusion.55
  599.9 0.9 copy-done.2
  600.8 1.0 fusion.52
  601.8 1.9 fusion.53
  603.7 2.9 fusion.55
  606.7 0.9 copy-done.2
  607.6 94.8 %collective-permute-start.3 = (bf16[768]{0:T(1024)(128)(2,1)S(1)}, bf16[768]{0:T(1024)(128)(2,1)S(1)}, u32[]{:S(2)}, u32[]{:S(2)}) collective-permute-start(bf16[768]{0:T(1024)(128)(2,1)S(1)} %slice.69), channel_id=1, source_target_pairs={{0,1},{1,0},{2,3},{3,2},{4,5},{5,4},{6,7},{7,6},{8,9},{9,8},{10,11... | collective-permute-start | bytes 4616 | tf_op jit(solution)/shard_map/ppermute | solution.py:22
  702.4 1.9 collective-permute-start.1
  704.3 1.0 slice.68
  705.3 2.4 collective-permute-start.2
  707.8 0.6 fusion.31
  708.4 0.4 collective-permute-done.2
  708.8 1.4 divide_convert_fusion
  710.2 0.2 copy.16
  710.3 0.8 copy.17
  (79 shorter events, 0.3 us)
Async XLA Ops:
  7.2 24.3 %copy-start = (bf16[128,2048]{1,0:T(8,128)(2,1)S(1)}, bf16[128,2048]{1,0:T(8,128)(2,1)}, u32[]{:S(2)}) copy-start(bf16[128,2048]{1,0:T(8,128)(2,1)} %param.10) | copy-start | bytes 1572868
  7.2 24.2 %copy-start.3 = (bf16[2048,64]{0,1:T(8,128)(2,1)S(1)}, bf16[2048,64]{0,1:T(8,128)(2,1)}, u32[]{:S(2)}) copy-start(bf16[2048,64]{0,1:T(8,128)(2,1)} %param.14) | copy-start | bytes 786436
  7.2 38.0 %copy-start.6 = (bf16[32,256]{1,0:T(8,128)(2,1)S(1)}, bf16[32,256]{1,0:T(8,128)(2,1)}, u32[]{:S(2)}) copy-start(bf16[32,256]{1,0:T(8,128)(2,1)} %param.16) | copy-start | bytes 49156
  7.2 39.5 %copy-start.5 = (bf16[32,768]{1,0:T(8,128)(2,1)S(1)}, bf16[32,768]{1,0:T(8,128)(2,1)}, u32[]{:S(2)}) copy-start(bf16[32,768]{1,0:T(8,128)(2,1)} %param.15) | copy-start | bytes 147460
  7.2 39.5 %copy-start.4 = (bf16[128,768]{1,0:T(8,128)(2,1)S(1)}, bf16[128,768]{1,0:T(8,128)(2,1)}, u32[]{:S(2)}) copy-start(bf16[128,768]{1,0:T(8,128)(2,1)} %param.11) | copy-start | bytes 589828
  7.2 45.2 %copy-start.7 = (s32[256]{0:T(256)S(1)}, s32[256]{0:T(256)}, u32[]{:S(2)}) copy-start(s32[256]{0:T(256)} %param.17) | copy-start | bytes 3076
  10.0 543.2 %all-to-all-start = ((bf16[128,64,128]{2,1,0:T(8,128)(2,1)}), bf16[128,64,128]{2,1,0:T(8,128)(2,1)S(1)}, u32[]{:S(2)}, u32[]{:S(2)}) async-start(bf16[128,64,128]{2,1,0:T(8,128)(2,1)} %stack.2), calls=%async_computation | async-start | bytes 4194304 | tf_op jit(solution)/shard_map/all_to_all | solution.py:17
  31.4 521.9 %all-gather.2.cloned.1.call-start = ((), (), s32[]{:S(2)}) async-start(), calls=%async_computation.1 | async-start | bytes 2113536 | tf_op jit(solution)/shard_map/all_gather | solution.py:147
  47.3 6.1 collective-permute-start
  554.3 1.9 copy-start.1
  559.2 0.9 copy-start.2
  561.1 1.9 copy-start.1
  565.9 0.9 copy-start.2
  567.9 1.9 copy-start.1
  572.7 0.9 copy-start.2
  574.6 1.9 copy-start.1
  579.5 0.9 copy-start.2
  581.4 1.9 copy-start.1
  586.3 0.9 copy-start.2
  588.2 1.9 copy-start.1
  593.1 0.9 copy-start.2
  595.0 1.9 copy-start.1
  599.9 0.9 copy-start.2
  601.8 1.9 copy-start.1
  606.7 0.9 copy-start.2
  607.6 100.2 %collective-permute-start.3 = (bf16[768]{0:T(1024)(128)(2,1)S(1)}, bf16[768]{0:T(1024)(128)(2,1)S(1)}, u32[]{:S(2)}, u32[]{:S(2)}) collective-permute-start(bf16[768]{0:T(1024)(128)(2,1)S(1)} %slice.69), channel_id=1, source_target_pairs={{0,1},{1,0},{2,3},{3,2},{4,5},{5,4},{6,7},{7,6},{8,9},{9,8},{10,11... | collective-permute-start | bytes 4616 | tf_op jit(solution)/shard_map/ppermute | solution.py:22
  702.4 5.4 collective-permute-start.1
  705.3 3.5 collective-permute-start.2
Sparse Core Ops, SparseCore 0:
  46.8 506.3 all-gather.1
